TPU v7x, 32 devices: a whole 2x2x4 slice. The times are simulated.
32 devices in a mesh: clip: 2 (over y), frame: 4 (over x, core), tensor: 4 (over z).
Axes of the slice: x: 2, y: 2, z: 4, core: 2. Of those that a mesh axis runs over, the one named last changes fastest.
Arguments:
- x_in: bfloat16 [2, 16, 256, 1152], P('clip', 'frame', 'tensor'), may hold values from -6 to 6
- cond: bfloat16 [2, 1152], P('clip'), may hold values from -6 to 6
- mod_weight_one: float32 [1152, 6, 1152], P(('clip', 'frame'), None, 'tensor'), may hold values from -0.1875 to 0.1875
- qkv_weight_one: float32 [1152, 3, 1152], P(('clip', 'frame'), None, 'tensor'), may hold values from -0.1875 to 0.1875
- attn_out_one: float32 [1152, 1152], P('tensor', ('clip', 'frame')), may hold values from -0.75 to 0.75
- mlp_up_one: float32 [1152, 4608], P(('clip', 'frame'), 'tensor'), may hold values from -0.1875 to 0.1875
- mlp_down_one: float32 [4608, 1152], P('tensor', ('clip', 'frame')), may hold values from -0.09375 to 0.09375
- mod_weight_two: float32 [1152, 6, 1152], P(('clip', 'frame'), None, 'tensor'), may hold values from -0.1875 to 0.1875
- qkv_weight_two: float32 [1152, 3, 1152], P(('clip', 'frame'), None, 'tensor'), may hold values from -0.1875 to 0.1875
- attn_out_two: float32 [1152, 1152], P('tensor', ('clip', 'frame')), may hold values from -0.375 to 0.375
- mlp_up_two: float32 [1152, 4608], P(('clip', 'frame'), 'tensor'), may hold values from -0.1875 to 0.1875
- mlp_down_two: float32 [4608, 1152], P('tensor', ('clip', 'frame')), may hold values from -0.09375 to 0.09375
- out_cotangent: bfloat16 [2, 16, 256, 1152], P('clip', 'frame', 'tensor'), may hold values from -6 to 6
Outputs:
- layer_out: bfloat16 [2, 16, 256, 1152], P('clip', 'frame', 'tensor')
- input_grad: float32 [2, 16, 256, 1152], P('clip', 'frame', 'tensor')
- cond_grad: float32 [2, 1152], P('clip')
- grad_mod_one: float32 [1152, 6, 1152], P(('clip', 'frame'), None, 'tensor')
- grad_qkv_one: float32 [1152, 3, 1152], P(('clip', 'frame'), None, 'tensor')
- grad_attn_one: float32 [1152, 1152], P('tensor', ('clip', 'frame'))
- grad_up_one: float32 [1152, 4608], P(('clip', 'frame'), 'tensor')
- grad_down_one: float32 [4608, 1152], P('tensor', ('clip', 'frame'))
- grad_mod_two: float32 [1152, 6, 1152], P(('clip', 'frame'), None, 'tensor')
- grad_qkv_two: float32 [1152, 3, 1152], P(('clip', 'frame'), None, 'tensor')
- grad_attn_two: float32 [1152, 1152], P('tensor', ('clip', 'frame'))
- grad_up_two: float32 [1152, 4608], P(('clip', 'frame'), 'tensor')
- grad_down_two: float32 [4608, 1152], P('tensor', ('clip', 'frame'))
All inputs are finite; a program needn't handle non-finite values.
Results may differ from a plain program's by a relative error of at most 0.02.
Values may be sent and summed in bfloat16 or wider, within the bound.
No kernel may reach another device: no remote copies, remote signals or barrier semaphores. Data moves between devices by JAX's collectives and lax.ppermute only.
A program may use at most 192 MiB of HBM per device.

v0:
```python
import jax
import jax.numpy as jnp
from jax import lax
from jax.sharding import PartitionSpec as P

HD = 72
HIGHEST_PRECISION = lax.Precision.HIGHEST
SCORE_FORMS = {True: "cfphe,cfqhe->cfhpq", False: "cfphe,cgphe->cphfg"}
APPLY_FORMS = {True: "cfhpq,cfqhe->cfphe", False: "cphfg,cgphe->cfphe"}
BACK_FORMS = {True: "cfhpq,cfphe->cfqhe", False: "cphfg,cfphe->cgphe"}
GELU_COEFF = 0.7978845608028654
CUBIC_COEFF = 0.044715


def layer_norm(stream):
    centre = stream - jnp.mean(stream, axis=-1, keepdims=True)
    inv_scale = lax.rsqrt(jnp.mean(centre * centre, axis=-1, keepdims=True) + 1e-06)
    return (centre * inv_scale, inv_scale)


def norm_back(normed, inv_scale, upstream):
    return inv_scale * (
        upstream
        - jnp.mean(upstream, axis=-1, keepdims=True)
        - normed * jnp.mean(upstream * normed, axis=-1, keepdims=True)
    )


def gelu_tanh(inputs):
    return (
        0.5
        * inputs
        * (1.0 + jnp.tanh(GELU_COEFF * (inputs + CUBIC_COEFF * inputs * inputs * inputs)))
    )


def gelu_slope(inputs):
    tangent = jnp.tanh(GELU_COEFF * (inputs + CUBIC_COEFF * inputs * inputs * inputs))
    return 0.5 * (1.0 + tangent) + 0.5 * inputs * (1.0 - tangent * tangent) * GELU_COEFF * (
        1.0 + 3.0 * CUBIC_COEFF * inputs * inputs
    )


def choose(modulation, column):
    return modulation[:, column][:, None, None, :]


def split_heads(projected):
    leading = projected.shape[:3]
    row_width = projected.shape[-1]
    head_count = row_width // HD
    queries = projected[:, :, :, 0].reshape(leading + (head_count, HD))
    key_rows = projected[:, :, :, 1].reshape(leading + (head_count, HD))
    values = projected[:, :, :, 2].reshape(leading + (head_count, HD))
    return (queries, key_rows, values, leading, row_width)


def attend(projected, spatial):
    queries, key_rows, values, leading, row_width = split_heads(projected)
    scores = jnp.einsum(
        SCORE_FORMS[spatial], queries, key_rows, preferred_element_type=jnp.float32
    ) * HD ** (-0.5)
    highest = jnp.max(scores, axis=-1, keepdims=True)
    expo = jnp.exp(scores - highest)
    denominator = jnp.sum(expo, axis=-1, keepdims=True)
    probs = (expo / denominator).astype(jnp.bfloat16)
    log_total = highest + jnp.log(denominator)
    attended = jnp.einsum(APPLY_FORMS[spatial], probs, values, preferred_element_type=jnp.float32)
    return (attended.reshape(leading + (row_width,)).astype(jnp.bfloat16), log_total)


def attend_back(projected, log_total, d_attended, spatial):
    queries, key_rows, values, leading, row_width = split_heads(projected)
    scale_factor = HD ** (-0.5)
    scores = (
        jnp.einsum(SCORE_FORMS[spatial], queries, key_rows, preferred_element_type=jnp.float32)
        * scale_factor
    )
    probs = jnp.exp(scores - log_total)
    upstream = d_attended.reshape(leading + (row_width // HD, HD))
    d_probs = jnp.einsum(SCORE_FORMS[spatial], upstream, values, preferred_element_type=jnp.float32)
    d_values = jnp.einsum(
        BACK_FORMS[spatial],
        probs.astype(jnp.bfloat16),
        upstream,
        preferred_element_type=jnp.float32,
    )
    row_inner = jnp.sum(probs * d_probs, axis=-1, keepdims=True)
    d_scores = (probs * (d_probs - row_inner)).astype(jnp.bfloat16)
    d_queries = (
        jnp.einsum(APPLY_FORMS[spatial], d_scores, key_rows, preferred_element_type=jnp.float32)
        * scale_factor
    )
    d_keys = (
        jnp.einsum(BACK_FORMS[spatial], d_scores, queries, preferred_element_type=jnp.float32)
        * scale_factor
    )
    stacked = jnp.stack([d_queries, d_keys, d_values], axis=3)
    return stacked.reshape(leading + (3, row_width)).astype(jnp.bfloat16)


def fetch_weights(weights):
    cast = tuple((weight.astype(jnp.bfloat16) for weight in weights))
    return (
        lax.all_gather(cast[0], ("clip", "frame"), axis=0, tiled=True),
        lax.all_gather(cast[1], ("clip", "frame"), axis=0, tiled=True),
        lax.all_gather(cast[2], ("clip", "frame"), axis=1, tiled=True),
        lax.all_gather(cast[3], ("clip", "frame"), axis=0, tiled=True),
        lax.all_gather(cast[4], ("clip", "frame"), axis=1, tiled=True),
    )


def backward_weights(weights):
    cast = tuple((weight.astype(jnp.bfloat16) for weight in weights))
    return (
        lax.all_gather(cast[0], ("clip", "frame"), axis=0, tiled=True),
        lax.all_gather(cast[1], ("clip", "frame"), axis=0, tiled=True),
        lax.all_gather(cast[2], ("clip", "frame"), axis=1, tiled=True),
        lax.all_gather(cast[3], ("clip", "frame"), axis=0, tiled=True),
        lax.all_gather(cast[4], ("clip", "frame"), axis=1, tiled=True),
    )


def spread_rows(rows):
    return lax.all_gather(rows, "tensor", axis=2, tiled=True)


def collect_rows(term):
    return lax.psum_scatter(term, "tensor", scatter_dimension=2, tiled=True)


def attention_output(attended, attn_weight):
    return collect_rows(
        jnp.einsum("cfpz,zd->cfpd", attended, attn_weight, preferred_element_type=jnp.float32)
    )


def layer_forward(stream, silu_cond, gathered, spatial):
    mod_weight, qkv_weight, attn_weight, up_weight, down_weight = gathered
    partial_value = jnp.einsum(
        "cd,dkz->ckz", silu_cond, mod_weight, preferred_element_type=jnp.float32
    )
    modulation = lax.all_gather(partial_value, "tensor", axis=2, tiled=True)
    normed, inv_scale = layer_norm(stream)
    modulated = (normed * (1.0 + choose(modulation, 1)) + choose(modulation, 0)).astype(
        jnp.bfloat16
    )
    gathered_rows = spread_rows(modulated)
    projected = jnp.einsum(
        "cfpd,dkz->cfpkz", gathered_rows, qkv_weight, preferred_element_type=jnp.float32
    ).astype(jnp.bfloat16)
    if spatial:
        project_held = projected
        attended, log_total = attend(project_held, True)
    else:
        project_held = lax.all_to_all(projected, "frame", split_axis=2, concat_axis=1, tiled=True)
        placed, log_total = attend(project_held, False)
        attended = lax.all_to_all(placed, "frame", split_axis=1, concat_axis=2, tiled=True)
    branch_attn = attention_output(attended, attn_weight)
    middle = stream + choose(modulation, 2) * branch_attn
    normed_mlp, inv_mlp = layer_norm(middle)
    modulated_mlp = (normed_mlp * (1.0 + choose(modulation, 4)) + choose(modulation, 3)).astype(
        jnp.bfloat16
    )
    gathered_mlp = spread_rows(modulated_mlp)
    hidden_pre = jnp.einsum(
        "cfpd,dz->cfpz", gathered_mlp, up_weight, preferred_element_type=jnp.float32
    )
    hidden_act = gelu_tanh(hidden_pre).astype(jnp.bfloat16)
    branch_mlp = collect_rows(
        jnp.einsum("cfpz,zd->cfpd", hidden_act, down_weight, preferred_element_type=jnp.float32)
    )
    result = middle + choose(modulation, 5) * branch_mlp
    stored = (
        modulation,
        normed,
        inv_scale,
        gathered_rows,
        project_held,
        log_total,
        attended,
        branch_attn,
        normed_mlp,
        inv_mlp,
        gathered_mlp,
        hidden_pre,
        hidden_act,
        branch_mlp,
    )
    return (result, stored)


def layer_backward(upstream, silu_cond, gathered, stored, spatial):
    mod_weight, qkv_weight, attn_weight, up_weight, down_weight = gathered
    (
        modulation,
        normed,
        inv_scale,
        gathered_rows,
        project_held,
        log_total,
        attended,
        branch_attn,
        normed_mlp,
        inv_mlp,
        gathered_mlp,
        hidden_pre,
        hidden_act,
        branch_mlp,
    ) = stored
    d_branch_mlp = (upstream * choose(modulation, 5)).astype(jnp.bfloat16)
    d_gate_mlp = jnp.sum(upstream * branch_mlp, axis=(1, 2))
    d_branch_all = spread_rows(d_branch_mlp)
    grad_down = jnp.einsum(
        "cfpz,cfpd->zd", hidden_act, d_branch_all, preferred_element_type=jnp.float32
    )
    d_act = jnp.einsum(
        "cfpd,zd->cfpz", d_branch_all, down_weight, preferred_element_type=jnp.float32
    )
    d_pre = (d_act * gelu_slope(hidden_pre)).astype(jnp.bfloat16)
    grad_up = jnp.einsum("cfpd,cfpz->dz", gathered_mlp, d_pre, preferred_element_type=jnp.float32)
    d_mod_mlp = collect_rows(
        jnp.einsum("cfpz,dz->cfpd", d_pre, up_weight, preferred_element_type=jnp.float32)
    )
    d_shift_mlp = jnp.sum(d_mod_mlp, axis=(1, 2))
    d_scale_mlp = jnp.sum(d_mod_mlp * normed_mlp, axis=(1, 2))
    d_middle = upstream + norm_back(normed_mlp, inv_mlp, d_mod_mlp * (1.0 + choose(modulation, 4)))
    d_branch_attn = (d_middle * choose(modulation, 2)).astype(jnp.bfloat16)
    d_gate_attn = jnp.sum(d_middle * branch_attn, axis=(1, 2))
    d_attn_all = spread_rows(d_branch_attn)
    grad_attn = jnp.einsum(
        "cfpz,cfpd->zd", attended, d_attn_all, preferred_element_type=jnp.float32
    )
    d_attended = jnp.einsum(
        "cfpd,zd->cfpz", d_attn_all, attn_weight, preferred_element_type=jnp.float32
    ).astype(jnp.bfloat16)
    if spatial:
        d_projected = attend_back(project_held, log_total, d_attended, True)
    else:
        d_placed = lax.all_to_all(d_attended, "frame", split_axis=2, concat_axis=1, tiled=True)
        d_projected = lax.all_to_all(
            attend_back(project_held, log_total, d_placed, False),
            "frame",
            split_axis=1,
            concat_axis=2,
            tiled=True,
        )
    grad_qkv = jnp.einsum(
        "cfpd,cfpkz->dkz", gathered_rows, d_projected, preferred_element_type=jnp.float32
    )
    d_modulated = collect_rows(
        jnp.einsum("cfpkz,dkz->cfpd", d_projected, qkv_weight, preferred_element_type=jnp.float32)
    )
    d_shift_attn = jnp.sum(d_modulated, axis=(1, 2))
    d_scale_attn = jnp.sum(d_modulated * normed, axis=(1, 2))
    d_stream = d_middle + norm_back(normed, inv_scale, d_modulated * (1.0 + choose(modulation, 1)))
    d_modulation = jnp.stack(
        [d_shift_attn, d_scale_attn, d_gate_attn, d_shift_mlp, d_scale_mlp, d_gate_mlp], axis=1
    )
    d_mod_own = lax.psum_scatter(d_modulation, "tensor", scatter_dimension=2, tiled=True)
    grad_mod = jnp.einsum(
        "cd,ckz->dkz", silu_cond.astype(jnp.float32), d_mod_own, precision=HIGHEST_PRECISION
    )
    d_silu = jnp.einsum(
        "ckz,dkz->cd", d_mod_own, mod_weight.astype(jnp.float32), precision=HIGHEST_PRECISION
    )
    grads = (
        lax.psum_scatter(
            grad_mod.astype(jnp.bfloat16), ("clip", "frame"), scatter_dimension=0, tiled=True
        ).astype(jnp.float32),
        lax.psum_scatter(
            grad_qkv.astype(jnp.bfloat16), ("clip", "frame"), scatter_dimension=0, tiled=True
        ).astype(jnp.float32),
        lax.psum_scatter(
            grad_attn.astype(jnp.bfloat16), ("clip", "frame"), scatter_dimension=1, tiled=True
        ).astype(jnp.float32),
        lax.psum_scatter(
            grad_up.astype(jnp.bfloat16), ("clip", "frame"), scatter_dimension=0, tiled=True
        ).astype(jnp.float32),
        lax.psum_scatter(
            grad_down.astype(jnp.bfloat16), ("clip", "frame"), scatter_dimension=1, tiled=True
        ).astype(jnp.float32),
    )
    return (d_stream, d_silu, grads)


def local(
    x_in,
    cond,
    mod_weight_one,
    qkv_weight_one,
    attn_out_one,
    mlp_up_one,
    mlp_down_one,
    mod_weight_two,
    qkv_weight_two,
    attn_out_two,
    mlp_up_two,
    mlp_down_two,
    out_cotangent,
):
    weights_first = (mod_weight_one, qkv_weight_one, attn_out_one, mlp_up_one, mlp_down_one)
    weights_second = (mod_weight_two, qkv_weight_two, attn_out_two, mlp_up_two, mlp_down_two)
    cond_float = cond.astype(jnp.float32)
    silu_cond = jax.nn.silu(cond_float).astype(jnp.bfloat16)
    gathered_first = fetch_weights(weights_first)
    middle_stream, stored_first = layer_forward(
        x_in.astype(jnp.float32), silu_cond, gathered_first, True
    )
    gathered_second = fetch_weights(weights_second)
    result, stored_second = layer_forward(middle_stream, silu_cond, gathered_second, False)
    back_second = backward_weights(weights_second)
    d_middle_stream, d_silu_second, grads_second = layer_backward(
        out_cotangent.astype(jnp.float32), silu_cond, back_second, stored_second, False
    )
    back_first = backward_weights(weights_first)
    input_grad, d_silu_first, grads_first = layer_backward(
        d_middle_stream, silu_cond, back_first, stored_first, True
    )
    d_silu_total = lax.psum(d_silu_first + d_silu_second, ("frame", "tensor"))
    sigmoid_cond = jax.nn.sigmoid(cond_float)
    cond_grad = d_silu_total * (sigmoid_cond * (1.0 + cond_float * (1.0 - sigmoid_cond)))
    return (
        result.astype(jnp.bfloat16),
        input_grad,
        cond_grad,
        grads_first[0],
        grads_first[1],
        grads_first[2],
        grads_first[3],
        grads_first[4],
        grads_second[0],
        grads_second[1],
        grads_second[2],
        grads_second[3],
        grads_second[4],
    )


def solution(mesh):
    return jax.shard_map(
        local,
        mesh=mesh,
        in_specs=(
            P("clip", "frame", "tensor", None),
            P("clip", None),
            P(("clip", "frame"), None, "tensor"),
            P(("clip", "frame"), None, "tensor"),
            P("tensor", ("clip", "frame")),
            P(("clip", "frame"), "tensor"),
            P("tensor", ("clip", "frame")),
            P(("clip", "frame"), None, "tensor"),
            P(("clip", "frame"), None, "tensor"),
            P("tensor", ("clip", "frame")),
            P(("clip", "frame"), "tensor"),
            P("tensor", ("clip", "frame")),
            P("clip", "frame", "tensor", None),
        ),
        out_specs=(
            P("clip", "frame", "tensor", None),
            P("clip", "frame", "tensor", None),
            P("clip", None),
            P(("clip", "frame"), None, "tensor"),
            P(("clip", "frame"), None, "tensor"),
            P("tensor", ("clip", "frame")),
            P(("clip", "frame"), "tensor"),
            P("tensor", ("clip", "frame")),
            P(("clip", "frame"), None, "tensor"),
            P(("clip", "frame"), None, "tensor"),
            P("tensor", ("clip", "frame")),
            P(("clip", "frame"), "tensor"),
            P("tensor", ("clip", "frame")),
        ),
        check_vma=False,
    )
```

profile of v0, /device:TPU:0, one launch (start us, length us, event | category | flops | bytes accessed | tf_op | source)
XLA Modules:
  0.0 2178.5 jit_solution(7276182978386951180)
XLA Ops:
  11.7 43.0 %all-gather.21.cloned.1.call-done = bf16[1152,6,288]{2,0,1:T(8,128)(2,1)} async-done(((bf16[144,6,288]{2,0,1:T(8,128)(2,1)}), bf16[1152,6,288]{2,0,1:T(8,128)(2,1)}) %all-gather.21.cloned.1.call-update) | async-done | bytes 3981328 | tf_op jit(solution)/shard_map/all_gather | solution.py:105
  89.8 52.6 %all-gather.23.cloned.1.call-done = bf16[1,4,256,1152]{3,2,1,0:T(8,128)(2,1)} async-done(((bf16[1,4,64,1152]{3,2,1,0:T(8,128)(2,1)}), bf16[1,4,256,1152]{3,2,1,0:T(8,128)(2,1)}) %all-gather.23.cloned.1.call-update) | async-done | bytes 2359312 | tf_op jit(solution)/shard_map/all_gather | solution.py:125
  156.9 82.4 %reduce-scatter.25.cloned.1.call-done = f32[1,4,64,1152]{3,2,1,0:T(8,128)} async-done(((f32[1,4,256,1152]{3,2,1,0:T(8,128)}), f32[1,4,64,1152]{3,2,1,0:T(8,128)}) %reduce-scatter.25.cloned.1.call-update) | async-done | bytes 1179664 | tf_op jit(solution)/shard_map/reduce_scatter | solution.py:129
  246.0 26.4 %all-gather.29.cloned.1.call-done = bf16[1152,1152]{1,0:T(8,128)(2,1)} async-done(((bf16[144,1152]{1,0:T(8,128)(2,1)}), bf16[1152,1152]{1,0:T(8,128)(2,1)}) %all-gather.29.cloned.1.call-update) | async-done | bytes 2654224 | tf_op jit(solution)/shard_map/all_gather | solution.py:108
  272.4 52.5 %all-gather.27.cloned.1.call-done = bf16[1,4,256,1152]{3,2,1,0:T(8,128)(2,1)} async-done(((bf16[1,4,64,1152]{3,2,1,0:T(8,128)(2,1)}), bf16[1,4,256,1152]{3,2,1,0:T(8,128)(2,1)}) %all-gather.27.cloned.1.call-update) | async-done | bytes 2359312 | tf_op jit(solution)/shard_map/all_gather | solution.py:125
  368.0 32.4 %all-gather.33.cloned.1.call-done = bf16[1152,6,288]{2,0,1:T(8,128)(2,1)} async-done(((bf16[144,6,288]{2,0,1:T(8,128)(2,1)}), bf16[1152,6,288]{2,0,1:T(8,128)(2,1)}) %all-gather.33.cloned.1.call-update) | async-done | bytes 3981328 | tf_op jit(solution)/shard_map/all_gather | solution.py:105
  418.2 70.3 %reduce-scatter.27.cloned.1.call-done = f32[1,4,64,1152]{3,2,1,0:T(8,128)} async-done(((f32[1,4,256,1152]{3,2,1,0:T(8,128)}), f32[1,4,64,1152]{3,2,1,0:T(8,128)}) %reduce-scatter.27.cloned.1.call-update) | async-done | bytes 1179664 | tf_op jit(solution)/shard_map/reduce_scatter | solution.py:129
  491.4 30.1 %all-gather.37.cloned.1.call-done = bf16[1152,3,288]{2,0,1:T(8,128)(2,1)} async-done(((bf16[144,3,288]{2,0,1:T(8,128)(2,1)}), bf16[1152,3,288]{2,0,1:T(8,128)(2,1)}) %all-gather.37.cloned.1.call-update) | async-done | bytes 1990672 | tf_op jit(solution)/shard_map/all_gather | solution.py:106
  521.5 52.6 %all-gather.35.cloned.1.call-done = bf16[1,4,256,1152]{3,2,1,0:T(8,128)(2,1)} async-done(((bf16[1,4,64,1152]{3,2,1,0:T(8,128)(2,1)}), bf16[1,4,256,1152]{3,2,1,0:T(8,128)(2,1)}) %all-gather.35.cloned.1.call-update) | async-done | bytes 2359312 | tf_op jit(solution)/shard_map/all_gather | solution.py:125
  584.2 31.2 %all_to_all.63 = bf16[1,4,256,3,288]{4,1,3,0,2:T(4,128)(2,1)S(1)} all-to-all(bf16[1,4,256,3,288]{4,1,3,0,2:T(4,128)(2,1)S(1)} %copy.135), channel_id=1, replica_groups=mesh['clip'=2,'frame'=4,'tensor'=4] {'frame'}, dimensions={2} | all-to-all | bytes 3538944 | tf_op jit(solution)/shard_map/all_to_all | solution.py:156
  662.3 81.6 %reduce-scatter.29.cloned.1.call-done = f32[1,4,64,1152]{3,2,1,0:T(8,128)} async-done(((f32[1,4,256,1152]{3,2,1,0:T(8,128)}), f32[1,4,64,1152]{3,2,1,0:T(8,128)}) %reduce-scatter.29.cloned.1.call-update) | async-done | bytes 1179664 | tf_op jit(solution)/shard_map/reduce_scatter | solution.py:129
  776.6 52.5 %all-gather.39.cloned.1.call-done = bf16[1,4,256,1152]{3,2,1,0:T(8,128)(2,1)} async-done(((bf16[1,4,64,1152]{3,2,1,0:T(8,128)(2,1)}), bf16[1,4,256,1152]{3,2,1,0:T(8,128)(2,1)}) %all-gather.39.cloned.1.call-update) | async-done | bytes 2359312 | tf_op jit(solution)/shard_map/all_gather | solution.py:125
  860.5 52.5 %all-gather.45.cloned.1.call-done = bf16[1,4,256,1152]{3,2,1,0:T(8,128)(2,1)} async-done(((bf16[1,4,64,1152]{3,2,1,0:T(8,128)(2,1)}), bf16[1,4,256,1152]{3,2,1,0:T(8,128)(2,1)}) %all-gather.45.cloned.1.call-update) | async-done | bytes 2359312 | tf_op jit(solution)/shard_map/all_gather | solution.py:125
  936.8 74.7 %reduce-scatter.33.cloned.1.call-done = f32[1,4,64,1152]{3,2,1,0:T(8,128)} async-done(((f32[1,4,256,1152]{3,2,1,0:T(8,128)}), f32[1,4,64,1152]{3,2,1,0:T(8,128)}) %reduce-scatter.33.cloned.1.call-update) | async-done | bytes 1179664 | tf_op jit(solution)/shard_map/reduce_scatter | solution.py:129
  1014.2 85.2 %reduce-scatter.31.cloned.1.call-done = f32[1,4,64,1152]{3,2,1,0:T(8,128)} async-done(((f32[1,4,256,1152]{3,2,1,0:T(8,128)}), f32[1,4,64,1152]{3,2,1,0:T(8,128)}) %reduce-scatter.31.cloned.1.call-update) | async-done | bytes 1179664 | tf_op jit(solution)/shard_map/reduce_scatter | solution.py:129
  1106.1 51.1 %all-gather.47.cloned.1.call-done = bf16[1,4,256,1152]{3,2,1,0:T(8,128)(2,1)} async-done(((bf16[1,4,64,1152]{3,2,1,0:T(8,128)(2,1)}), bf16[1,4,256,1152]{3,2,1,0:T(8,128)(2,1)}) %all-gather.47.cloned.1.call-update) | async-done | bytes 2359312 | tf_op jit(solution)/shard_map/all_gather | solution.py:125
  1204.7 31.1 %all_to_all.64 = bf16[1,16,64,3,288]{4,2,3,0,1:T(8,128)(2,1)S(1)} all-to-all(bf16[1,16,64,3,288]{4,2,3,0,1:T(8,128)(2,1)S(1)} %copy.158), channel_id=1, replica_groups=mesh['clip'=2,'frame'=4,'tensor'=4] {'frame'}, dimensions={1} | all-to-all | bytes 3538944 | tf_op jit(solution)/shard_map/all_to_all | solution.py:241
  1243.8 83.3 %reduce-scatter.35.cloned.1.call-done = f32[1,4,64,1152]{3,2,1,0:T(8,128)} async-done(((f32[1,4,256,1152]{3,2,1,0:T(8,128)}), f32[1,4,64,1152]{3,2,1,0:T(8,128)}) %reduce-scatter.35.cloned.1.call-update) | async-done | bytes 1179664 | tf_op jit(solution)/shard_map/reduce_scatter | solution.py:129
  1333.0 51.1 %all-gather.49.cloned.1.call-done = bf16[1,4,256,1152]{3,2,1,0:T(8,128)(2,1)} async-done(((bf16[1,4,64,1152]{3,2,1,0:T(8,128)(2,1)}), bf16[1,4,256,1152]{3,2,1,0:T(8,128)(2,1)}) %all-gather.49.cloned.1.call-update) | async-done | bytes 2359312 | tf_op jit(solution)/shard_map/all_gather | solution.py:125
  1398.4 84.2 %reduce-scatter.37.cloned.1.call-done = f32[1,4,64,1152]{3,2,1,0:T(8,128)} async-done(((f32[1,4,256,1152]{3,2,1,0:T(8,128)}), f32[1,4,64,1152]{3,2,1,0:T(8,128)}) %reduce-scatter.37.cloned.1.call-update) | async-done | bytes 1179664 | tf_op jit(solution)/shard_map/reduce_scatter | solution.py:129
  1488.7 50.8 %all-gather.51.cloned.1.call-done = bf16[1,4,256,1152]{3,2,1,0:T(8,128)(2,1)} async-done(((bf16[1,4,64,1152]{3,2,1,0:T(8,128)(2,1)}), bf16[1,4,256,1152]{3,2,1,0:T(8,128)(2,1)}) %all-gather.51.cloned.1.call-update) | async-done | bytes 2359312 | tf_op jit(solution)/shard_map/all_gather | solution.py:125
  1556.4 82.2 %reduce-scatter.39.cloned.1.call-done = f32[1,4,64,1152]{3,2,1,0:T(8,128)} async-done(((f32[1,4,256,1152]{3,2,1,0:T(8,128)}), f32[1,4,64,1152]{3,2,1,0:T(8,128)}) %reduce-scatter.39.cloned.1.call-update) | async-done | bytes 1179664 | tf_op jit(solution)/shard_map/reduce_scatter | solution.py:129
  1707.4 25.1 %reduce-scatter.57.cloned.1.call-done = bf16[144,1152]{1,0:T(8,128)(2,1)} async-done(((bf16[1152,1152]{1,0:T(8,128)(2,1)}), bf16[144,1152]{1,0:T(8,128)(2,1)}) %reduce-scatter.57.cloned.1.call-update) | async-done | bytes 331792 | tf_op jit(solution)/shard_map/reduce_scatter | solution.py:277
  1734.3 45.8 %reduce-scatter.59.cloned.1.call-done = bf16[1152,144]{0,1:T(8,128)(2,1)} async-done(((bf16[1152,1152]{0,1:T(8,128)(2,1)}), bf16[1152,144]{0,1:T(8,128)(2,1)}) %reduce-scatter.59.cloned.1.call-update) | async-done | bytes 331792 | tf_op jit(solution)/shard_map/reduce_scatter | solution.py:280
  1782.0 37.1 %reduce-scatter.55.cloned.1.call-done = bf16[288,144]{0,1:T(8,128)(2,1)} async-done(((bf16[288,1152]{0,1:T(8,128)(2,1)}), bf16[288,144]{0,1:T(8,128)(2,1)}) %reduce-scatter.55.cloned.1.call-update) | async-done | bytes 82960 | tf_op jit(solution)/shard_map/reduce_scatter | solution.py:274
  1820.7 45.9 %reduce-scatter.53.cloned.1.call-done = bf16[144,3,288]{2,0,1:T(8,128)(2,1)} async-done(((bf16[1152,3,288]{2,0,1:T(8,128)(2,1)}), bf16[144,3,288]{2,0,1:T(8,128)(2,1)}) %reduce-scatter.53.cloned.1.call-update) | async-done | bytes 248848 | tf_op jit(solution)/shard_map/reduce_scatter | solution.py:271
  1875.2 38.7 %reduce-scatter.47.cloned.1.call-done = bf16[144,1152]{1,0:T(8,128)(2,1)} async-done(((bf16[1152,1152]{1,0:T(8,128)(2,1)}), bf16[144,1152]{1,0:T(8,128)(2,1)}) %reduce-scatter.47.cloned.1.call-update) | async-done | bytes 331792 | tf_op jit(solution)/shard_map/reduce_scatter | solution.py:277
  1915.8 45.8 %reduce-scatter.49.cloned.1.call-done = bf16[1152,144]{0,1:T(8,128)(2,1)} async-done(((bf16[1152,1152]{0,1:T(8,128)(2,1)}), bf16[1152,144]{0,1:T(8,128)(2,1)}) %reduce-scatter.49.cloned.1.call-update) | async-done | bytes 331792 | tf_op jit(solution)/shard_map/reduce_scatter | solution.py:280
  1963.4 36.9 %reduce-scatter.45.cloned.1.call-done = bf16[288,144]{0,1:T(8,128)(2,1)} async-done(((bf16[288,1152]{0,1:T(8,128)(2,1)}), bf16[288,144]{0,1:T(8,128)(2,1)}) %reduce-scatter.45.cloned.1.call-update) | async-done | bytes 82960 | tf_op jit(solution)/shard_map/reduce_scatter | solution.py:274
  2001.9 46.1 %reduce-scatter.43.cloned.1.call-done = bf16[144,3,288]{2,0,1:T(8,128)(2,1)} async-done(((bf16[1152,3,288]{2,0,1:T(8,128)(2,1)}), bf16[144,3,288]{2,0,1:T(8,128)(2,1)}) %reduce-scatter.43.cloned.1.call-update) | async-done | bytes 248848 | tf_op jit(solution)/shard_map/reduce_scatter | solution.py:271
  2058.1 34.4 %psum.7 = f32[1,1152]{1,0:T(1,128)S(1)} all-reduce(f32[1,1152]{1,0:T(1,128)S(1)} %add.296), channel_id=1, replica_groups=mesh['clip'=2,'frame'=4,'tensor'=4] {'frame','tensor'}, use_global_device_ids=true, to_apply=%region_44.45 | all-reduce | flops 1152 | bytes 9216 | tf_op jit(solution)/shard_map/psum | solution.py:320
  2111.1 58.4 %reduce-scatter.51.cloned.1.call-done = bf16[144,6,288]{2,0,1:T(8,128)(2,1)} async-done(((bf16[1152,6,288]{2,0,1:T(8,128)(2,1)}), bf16[144,6,288]{2,0,1:T(8,128)(2,1)}) %reduce-scatter.51.cloned.1.call-update) | async-done | bytes 497680 | tf_op jit(solution)/shard_map/reduce_scatter | solution.py:268
  (424 shorter events, 495.0 us)
Async XLA Ops:
  10.5 132.0 %all-gather.23.cloned.1.call-start = ((), (), s32[]{:S(2)}) async-start(), calls=%async_computation.25 | async-start | bytes 2949120 | tf_op jit(solution)/shard_map/all_gather | solution.py:125
  73.1 166.2 %reduce-scatter.25.cloned.1.call-start = ((), (), s32[]{:S(2)}) async-start(), calls=%async_computation.27 | async-start | bytes 5898240 | tf_op jit(solution)/shard_map/reduce_scatter | solution.py:129
  155.0 117.4 %all-gather.29.cloned.1.call-start = ((), (), s32[]{:S(2)}) async-start(), calls=%async_computation.29 | async-start | bytes 2985984 | tf_op jit(solution)/shard_map/all_gather | solution.py:108
  156.9 168.0 %all-gather.27.cloned.1.call-start = ((), (), s32[]{:S(2)}) async-start(), calls=%async_computation.28 | async-start | bytes 2949120 | tf_op jit(solution)/shard_map/all_gather | solution.py:125
  242.2 114.2 %all-gather.31.cloned.1.call-start = ((), (), s32[]{:S(2)}) async-start(), calls=%async_computation.30 | async-start | bytes 2985984 | tf_op jit(solution)/shard_map/all_gather | solution.py:109
  243.2 157.2 %all-gather.33.cloned.1.call-start = ((), (), s32[]{:S(2)}) async-start(), calls=%async_computation.32 | async-start | bytes 5971968 | tf_op jit(solution)/shard_map/all_gather | solution.py:105
  245.5 243.0 %reduce-scatter.27.cloned.1.call-start = ((), (), s32[]{:S(2)}) async-start(), calls=%async_computation.31 | async-start | bytes 5898240 | tf_op jit(solution)/shard_map/reduce_scatter | solution.py:129
  366.0 155.5 %all-gather.37.cloned.1.call-start = ((), (), s32[]{:S(2)}) async-start(), calls=%async_computation.34 | async-start | bytes 2985984 | tf_op jit(solution)/shard_map/all_gather | solution.py:106
  367.9 206.2 %all-gather.35.cloned.1.call-start = ((), (), s32[]{:S(2)}) async-start(), calls=%async_computation.33 | async-start | bytes 2949120 | tf_op jit(solution)/shard_map/all_gather | solution.py:125
  660.4 116.2 %all-gather.41.cloned.1.call-start = ((), (), s32[]{:S(2)}) async-start(), calls=%async_computation.37 | async-start | bytes 2985984 | tf_op jit(solution)/shard_map/all_gather | solution.py:108
  662.3 166.8 %all-gather.39.cloned.1.call-start = ((), (), s32[]{:S(2)}) async-start(), calls=%async_computation.36 | async-start | bytes 2949120 | tf_op jit(solution)/shard_map/all_gather | solution.py:125
  747.5 112.9 %all-gather.43.cloned.1.call-start = ((), (), s32[]{:S(2)}) async-start(), calls=%async_computation.38 | async-start | bytes 2985984 | tf_op jit(solution)/shard_map/all_gather | solution.py:109
  749.5 163.5 %all-gather.45.cloned.1.call-start = ((), (), s32[]{:S(2)}) async-start(), calls=%async_computation.40 | async-start | bytes 2949120 | tf_op jit(solution)/shard_map/all_gather | solution.py:125
  751.5 260.0 %reduce-scatter.33.cloned.1.call-start = ((), (), s32[]{:S(2)}) async-start(), calls=%async_computation.41 | async-start | bytes 5898240 | tf_op jit(solution)/shard_map/reduce_scatter | solution.py:129
  927.3 172.2 %reduce-scatter.31.cloned.1.call-start = ((), (), s32[]{:S(2)}) async-start(), calls=%async_computation.39 | async-start | bytes 5898240 | tf_op jit(solution)/shard_map/reduce_scatter | solution.py:129
  936.8 220.4 %all-gather.47.cloned.1.call-start = ((), (), s32[]{:S(2)}) async-start(), calls=%async_computation.42 | async-start | bytes 2949120 | tf_op jit(solution)/shard_map/all_gather | solution.py:125
  1167.2 159.9 %reduce-scatter.35.cloned.1.call-start = ((), (), s32[]{:S(2)}) async-start(), calls=%async_computation.43 | async-start | bytes 5898240 | tf_op jit(solution)/shard_map/reduce_scatter | solution.py:129
  1243.8 140.3 %all-gather.49.cloned.1.call-start = ((), (), s32[]{:S(2)}) async-start(), calls=%async_computation.44 | async-start | bytes 2949120 | tf_op jit(solution)/shard_map/all_gather | solution.py:125
  1332.9 149.7 %reduce-scatter.37.cloned.1.call-start = ((), (), s32[]{:S(2)}) async-start(), calls=%async_computation.45 | async-start | bytes 5898240 | tf_op jit(solution)/shard_map/reduce_scatter | solution.py:129
  1398.3 141.2 %all-gather.51.cloned.1.call-start = ((), (), s32[]{:S(2)}) async-start(), calls=%async_computation.46 | async-start | bytes 2949120 | tf_op jit(solution)/shard_map/all_gather | solution.py:125
  1488.4 150.2 %reduce-scatter.39.cloned.1.call-start = ((), (), s32[]{:S(2)}) async-start(), calls=%async_computation.47 | async-start | bytes 5898240 | tf_op jit(solution)/shard_map/reduce_scatter | solution.py:129
  1554.3 143.7 %reduce-scatter.63.cloned.1.call-start = ((), (), s32[]{:S(2)}) async-start(), calls=%async_computation.59 | async-start | bytes 737280
  1556.2 142.8 %reduce-scatter.61.cloned.1.call-start = ((), (), s32[]{:S(2)}) async-start(), calls=%async_computation.58 | async-start | bytes 737280
  1648.9 131.2 %reduce-scatter.59.cloned.1.call-start = ((), (), s32[]{:S(2)}) async-start(), calls=%async_computation.57 | async-start | bytes 2985984 | tf_op jit(solution)/shard_map/reduce_scatter | solution.py:280
  1657.5 161.6 %reduce-scatter.55.cloned.1.call-start = ((), (), s32[]{:S(2)}) async-start(), calls=%async_computation.55 | async-start | bytes 995328 | tf_op jit(solution)/shard_map/reduce_scatter | solution.py:274
  1662.6 204.0 %reduce-scatter.53.cloned.1.call-start = ((), (), s32[]{:S(2)}) async-start(), calls=%async_computation.54 | async-start | bytes 2985984 | tf_op jit(solution)/shard_map/reduce_scatter | solution.py:271
  1669.8 244.1 %reduce-scatter.47.cloned.1.call-start = ((), (), s32[]{:S(2)}) async-start(), calls=%async_computation.51 | async-start | bytes 2985984 | tf_op jit(solution)/shard_map/reduce_scatter | solution.py:277
  1677.2 284.4 %reduce-scatter.49.cloned.1.call-start = ((), (), s32[]{:S(2)}) async-start(), calls=%async_computation.52 | async-start | bytes 2985984 | tf_op jit(solution)/shard_map/reduce_scatter | solution.py:280
  1685.4 314.9 %reduce-scatter.45.cloned.1.call-start = ((), (), s32[]{:S(2)}) async-start(), calls=%async_computation.50 | async-start | bytes 995328 | tf_op jit(solution)/shard_map/reduce_scatter | solution.py:274
  1690.5 357.5 %reduce-scatter.43.cloned.1.call-start = ((), (), s32[]{:S(2)}) async-start(), calls=%async_computation.49 | async-start | bytes 2985984 | tf_op jit(solution)/shard_map/reduce_scatter | solution.py:271
  1697.3 411.6 %reduce-scatter.41.cloned.1.call-start = ((), (), s32[]{:S(2)}) async-start(), calls=%async_computation.48 | async-start | bytes 5971968 | tf_op jit(solution)/shard_map/reduce_scatter | solution.py:268
  1706.8 462.7 %reduce-scatter.51.cloned.1.call-start = ((), (), s32[]{:S(2)}) async-start(), calls=%async_computation.53 | async-start | bytes 5971968 | tf_op jit(solution)/shard_map/reduce_scatter | solution.py:268
  (94 other events, 3726.8 us)
Sparse Core Ops, SparseCore 0:
  10.5 44.0 all-gather.20
  57.1 32.6 all-gather.24
  91.9 50.4 all-gather.22
  155.2 84.0 reduce-scatter.24
  241.6 30.7 all-gather.28
  274.4 50.4 all-gather.26
  359.0 41.3 all-gather.32
  402.7 85.7 reduce-scatter.26
  490.8 30.5 all-gather.36
  523.6 50.4 all-gather.34
  660.5 83.3 reduce-scatter.28
  745.8 30.7 all-gather.40
  778.6 50.4 all-gather.38
  862.5 50.4 all-gather.44
  927.4 84.0 reduce-scatter.32
  1013.7 85.7 reduce-scatter.30
  1106.2 50.9 all-gather.46
  1243.9 83.1 reduce-scatter.34
  1333.1 50.9 all-gather.48
  1398.5 84.0 reduce-scatter.36
  1488.5 50.9 all-gather.50
  1554.4 84.0 reduce-scatter.38
  1690.4 42.0 reduce-scatter.56
  1736.3 43.7 reduce-scatter.58
  1783.9 35.0 reduce-scatter.54
  1822.8 43.7 reduce-scatter.52
  1870.1 43.7 reduce-scatter.46
  1917.8 43.7 reduce-scatter.48
  1965.2 35.0 reduce-scatter.44
  2004.2 43.7 reduce-scatter.42
  2051.5 57.3 reduce-scatter.40
  2112.3 57.2 reduce-scatter.50
  (4 shorter events, 100.8 us)
where the time goes:
time: 2190 us; the launch traced here: 2180 us
  waiting for transfers between devices  1670 us (76%)
  matrix products  185 us (8%)
  blocking collectives  155 us (7%)
  other arithmetic  81.1 us (4%)
  local copies, waits for them, and re-layouts  56.7 us (3%)
    reduce_scatter x8, waiting for transfers between devices, collect_rows(): return lax.psum_scatter(term, 'tensor', scatter_dimension=2, tiled=True)  644 us
    all_gather x8, waiting for transfers between devices, spread_rows(): return lax.all_gather(rows, 'tensor', axis=2, tiled=True)  416 us
    reduce_scatter x2, waiting for transfers between devices, layer_backward(): lax.psum_scatter(grad_qkv.astype(jnp.bfloat16), ('clip', 'frame'), scatte...  92 us
    reduce_scatter x2, waiting for transfers between devices, layer_backward(): lax.psum_scatter(grad_down.astype(jnp.bfloat16), ('clip', 'frame'), scatt...  91.6 us
    all_gather x2, waiting for transfers between devices, fetch_weights(): lax.all_gather(cast[0], ('clip', 'frame'), axis=0, tiled=True)  75.4 us
    reduce_scatter x2, waiting for transfers between devices, layer_backward(): lax.psum_scatter(grad_mod.astype(jnp.bfloat16), ('clip', 'frame'), scatte...  74.1 us
    reduce_scatter x2, waiting for transfers between devices, layer_backward(): lax.psum_scatter(grad_attn.astype(jnp.bfloat16), ('clip', 'frame'), scatt...  74 us
    reduce_scatter x2, waiting for transfers between devices, layer_backward(): lax.psum_scatter(grad_up.astype(jnp.bfloat16), ('clip', 'frame'), scatter...  63.8 us
  transfers between devices with their start and end apart: 38, of which 35 were waited for; matrix products, arithmetic and copies ran while one was open for 8% of the time, Pallas kernels for 0%

commit v1 on v0

--- a/solution.py
+++ b/solution.py
@@ -2,6 +2,7 @@
 import jax.numpy as jnp
 from jax import lax
 from jax.sharding import PartitionSpec as P
+from jax.lax import axis_index, axis_size, ppermute
 
 HD = 72
 HIGHEST_PRECISION = lax.Precision.HIGHEST
@@ -10,6 +11,29 @@
 BACK_FORMS = {True: "cfhpq,cfphe->cfqhe", False: "cphfg,cfphe->cgphe"}
 GELU_COEFF = 0.7978845608028654
 CUBIC_COEFF = 0.044715
+
+
+def turn_the_outputs(view, axis_no):
+    view = jnp.moveaxis(view, 0, axis_no)
+    d_next = view.shape
+    return view.reshape(
+        *d_next[:axis_no], d_next[axis_no] * d_next[axis_no + 1], *d_next[axis_no + 2 :]
+    )
+
+
+def stages_all_choose(block_here, row_axis):
+    y1, state_now = (axis_size(row_axis), axis_index(row_axis))
+    y2, part_now = (block_here[None], 1)
+    while part_now < y1:
+        w1 = ppermute(y2, row_axis, [(dev_i, dev_i ^ part_now) for dev_i in range(y1)])
+        f_now = state_now & part_now == 0
+        y2 = jnp.concatenate([jnp.where(f_now, y2, w1), jnp.where(f_now, w1, y2)])
+        part_now *= 2
+    return y2
+
+
+def step_on_cycles_for(z, s0, which_dim):
+    return turn_the_outputs(stages_all_choose(z, s0), which_dim)
 
 
 def layer_norm(stream):
@@ -102,7 +126,7 @@
 def fetch_weights(weights):
     cast = tuple((weight.astype(jnp.bfloat16) for weight in weights))
     return (
-        lax.all_gather(cast[0], ("clip", "frame"), axis=0, tiled=True),
+        step_on_cycles_for(cast[0], ("clip", "frame"), which_dim=0),
         lax.all_gather(cast[1], ("clip", "frame"), axis=0, tiled=True),
         lax.all_gather(cast[2], ("clip", "frame"), axis=1, tiled=True),
         lax.all_gather(cast[3], ("clip", "frame"), axis=0, tiled=True),

time: 2190 us -> 2320 us (1.059)
  waiting for transfers between devices: 1670 us -> 1780 us
    ppermute x0 -> x6, waiting for transfers between devices: none -> 181 us  [stages_all_choose(): ppermute(y2, row_axis, [(dev_i, dev_i ^ part_now) for dev_i in range(y1)])]
    reduce_scatter x8, waiting for transfers between devices: 644 us -> 574 us  [collect_rows(): return lax.psum_scatter(term, 'tensor', scatter_dimension=2, tiled=True)]
  transfers between devices with their start and end apart: 38 -> 44, of which waited for: 35 -> 39; matrix products, arithmetic and copies ran while one was open for 8% -> 7% of each run, Pallas kernels for 0% -> 0%
where the time goes in v1:
time: 2320 us; the launch traced here: 2310 us
  waiting for transfers between devices  1780 us (77%)
  matrix products  183 us (8%)
  blocking collectives  155 us (7%)
  other arithmetic  102 us (4%)
  local copies, waits for them, and re-layouts  56.5 us (2%)
    reduce_scatter x8, waiting for transfers between devices, collect_rows(): return lax.psum_scatter(term, 'tensor', scatter_dimension=2, tiled=True)  574 us
    all_gather x8, waiting for transfers between devices, spread_rows(): return lax.all_gather(rows, 'tensor', axis=2, tiled=True)  403 us
    ppermute x6, waiting for transfers between devices, stages_all_choose(): ppermute(y2, row_axis, [(dev_i, dev_i ^ part_now) for dev_i in range(y1)])  181 us
    reduce_scatter x2, waiting for transfers between devices, layer_backward(): lax.psum_scatter(grad_qkv.astype(jnp.bfloat16), ('clip', 'frame'), scatte...  92 us
    reduce_scatter x2, waiting for transfers between devices, layer_backward(): lax.psum_scatter(grad_down.astype(jnp.bfloat16), ('clip', 'frame'), scatt...  86 us
    all_gather x2, waiting for transfers between devices, backward_weights(): lax.all_gather(cast[0], ('clip', 'frame'), axis=0, tiled=True)  82.6 us
    reduce_scatter x2, waiting for transfers between devices, layer_backward(): lax.psum_scatter(grad_mod.astype(jnp.bfloat16), ('clip', 'frame'), scatte...  76.9 us
    reduce_scatter x2, waiting for transfers between devices, layer_backward(): lax.psum_scatter(grad_attn.astype(jnp.bfloat16), ('clip', 'frame'), scatt...  74.1 us
  transfers between devices with their start and end apart: 44, of which 39 were waited for; matrix products, arithmetic and copies ran while one was open for 7% of the time, Pallas kernels for 0%

profile of v1, /device:TPU:0, one launch (start us, length us, event | category | flops | bytes accessed | tf_op | source)
XLA Modules:
  0.0 2310.1 jit_solution(11917361715559464967)
XLA Ops:
  85.1 66.3 %collective-permute-done.2 = bf16[4,144,6,288]{3,1,2,0:T(8,128)(2,1)} collective-permute-done((bf16[4,144,6,288]{3,1,2,0:T(8,128)(2,1)}, bf16[4,144,6,288]{3,1,2,0:T(8,128)(2,1)}, u32[]{:S(2)}, u32[]{:S(2)}) %collective-permute-start.2) | collective-permute-done | bytes 1990688 | tf_op jit(solution)/shard_map/ppermute | solution.py:28
  182.2 40.6 %all-gather.21.cloned.1.call-done = bf16[1,4,256,1152]{3,2,1,0:T(8,128)(2,1)} async-done(((bf16[1,4,64,1152]{3,2,1,0:T(8,128)(2,1)}), bf16[1,4,256,1152]{3,2,1,0:T(8,128)(2,1)}) %all-gather.21.cloned.1.call-update) | async-done | bytes 2359312 | tf_op jit(solution)/shard_map/all_gather | solution.py:149
  237.2 82.4 %reduce-scatter.25.cloned.1.call-done = f32[1,4,64,1152]{3,2,1,0:T(8,128)} async-done(((f32[1,4,256,1152]{3,2,1,0:T(8,128)}), f32[1,4,64,1152]{3,2,1,0:T(8,128)}) %reduce-scatter.25.cloned.1.call-update) | async-done | bytes 1179664 | tf_op jit(solution)/shard_map/reduce_scatter | solution.py:153
  324.0 28.7 %all-gather.27.cloned.1.call-done = bf16[1152,1152]{1,0:T(8,128)(2,1)} async-done(((bf16[144,1152]{1,0:T(8,128)(2,1)}), bf16[1152,1152]{1,0:T(8,128)(2,1)}) %all-gather.27.cloned.1.call-update) | async-done | bytes 2654224 | tf_op jit(solution)/shard_map/all_gather | solution.py:132
  352.7 52.5 %all-gather.25.cloned.1.call-done = bf16[1,4,256,1152]{3,2,1,0:T(8,128)(2,1)} async-done(((bf16[1,4,64,1152]{3,2,1,0:T(8,128)(2,1)}), bf16[1,4,256,1152]{3,2,1,0:T(8,128)(2,1)}) %all-gather.25.cloned.1.call-update) | async-done | bytes 2359312 | tf_op jit(solution)/shard_map/all_gather | solution.py:149
  452.2 57.8 %collective-permute-done.5 = bf16[4,144,6,288]{3,1,2,0:T(8,128)(2,1)} collective-permute-done((bf16[4,144,6,288]{3,1,2,0:T(8,128)(2,1)}, bf16[4,144,6,288]{3,1,2,0:T(8,128)(2,1)}, u32[]{:S(2)}, u32[]{:S(2)}) %collective-permute-start.5) | collective-permute-done | bytes 1990688 | tf_op jit(solution)/shard_map/ppermute | solution.py:28
  535.2 30.4 %all-gather.33.cloned.1.call-done = bf16[1152,3,288]{2,0,1:T(8,128)(2,1)} async-done(((bf16[144,3,288]{2,0,1:T(8,128)(2,1)}), bf16[1152,3,288]{2,0,1:T(8,128)(2,1)}) %all-gather.33.cloned.1.call-update) | async-done | bytes 1990672 | tf_op jit(solution)/shard_map/all_gather | solution.py:130
  565.6 52.6 %all-gather.31.cloned.1.call-done = bf16[1,4,256,1152]{3,2,1,0:T(8,128)(2,1)} async-done(((bf16[1,4,64,1152]{3,2,1,0:T(8,128)(2,1)}), bf16[1,4,256,1152]{3,2,1,0:T(8,128)(2,1)}) %all-gather.31.cloned.1.call-update) | async-done | bytes 2359312 | tf_op jit(solution)/shard_map/all_gather | solution.py:149
  628.4 31.1 %all_to_all.63 = bf16[1,4,256,3,288]{4,1,3,0,2:T(4,128)(2,1)S(1)} all-to-all(bf16[1,4,256,3,288]{4,1,3,0,2:T(4,128)(2,1)S(1)} %copy.141), channel_id=1, replica_groups=mesh['clip'=2,'frame'=4,'tensor'=4] {'frame'}, dimensions={2} | all-to-all | bytes 3538944 | tf_op jit(solution)/shard_map/all_to_all | solution.py:180
  706.4 81.5 %reduce-scatter.29.cloned.1.call-done = f32[1,4,64,1152]{3,2,1,0:T(8,128)} async-done(((f32[1,4,256,1152]{3,2,1,0:T(8,128)}), f32[1,4,64,1152]{3,2,1,0:T(8,128)}) %reduce-scatter.29.cloned.1.call-update) | async-done | bytes 1179664 | tf_op jit(solution)/shard_map/reduce_scatter | solution.py:153
  821.2 52.5 %all-gather.35.cloned.1.call-done = bf16[1,4,256,1152]{3,2,1,0:T(8,128)(2,1)} async-done(((bf16[1,4,64,1152]{3,2,1,0:T(8,128)(2,1)}), bf16[1,4,256,1152]{3,2,1,0:T(8,128)(2,1)}) %all-gather.35.cloned.1.call-update) | async-done | bytes 2359312 | tf_op jit(solution)/shard_map/all_gather | solution.py:149
  905.3 52.5 %all-gather.41.cloned.1.call-done = bf16[1,4,256,1152]{3,2,1,0:T(8,128)(2,1)} async-done(((bf16[1,4,64,1152]{3,2,1,0:T(8,128)(2,1)}), bf16[1,4,256,1152]{3,2,1,0:T(8,128)(2,1)}) %all-gather.41.cloned.1.call-update) | async-done | bytes 2359312 | tf_op jit(solution)/shard_map/all_gather | solution.py:149
  981.8 74.5 %reduce-scatter.33.cloned.1.call-done = f32[1,4,64,1152]{3,2,1,0:T(8,128)} async-done(((f32[1,4,256,1152]{3,2,1,0:T(8,128)}), f32[1,4,64,1152]{3,2,1,0:T(8,128)}) %reduce-scatter.33.cloned.1.call-update) | async-done | bytes 1179664 | tf_op jit(solution)/shard_map/reduce_scatter | solution.py:153
  1059.0 85.2 %reduce-scatter.31.cloned.1.call-done = f32[1,4,64,1152]{3,2,1,0:T(8,128)} async-done(((f32[1,4,256,1152]{3,2,1,0:T(8,128)}), f32[1,4,64,1152]{3,2,1,0:T(8,128)}) %reduce-scatter.31.cloned.1.call-update) | async-done | bytes 1179664 | tf_op jit(solution)/shard_map/reduce_scatter | solution.py:153
  1150.8 51.1 %all-gather.43.cloned.1.call-done = bf16[1,4,256,1152]{3,2,1,0:T(8,128)(2,1)} async-done(((bf16[1,4,64,1152]{3,2,1,0:T(8,128)(2,1)}), bf16[1,4,256,1152]{3,2,1,0:T(8,128)(2,1)}) %all-gather.43.cloned.1.call-update) | async-done | bytes 2359312 | tf_op jit(solution)/shard_map/all_gather | solution.py:149
  1248.6 31.2 %all_to_all.64 = bf16[1,16,64,3,288]{4,2,3,0,1:T(8,128)(2,1)S(1)} all-to-all(bf16[1,16,64,3,288]{4,2,3,0,1:T(8,128)(2,1)S(1)} %copy.164), channel_id=1, replica_groups=mesh['clip'=2,'frame'=4,'tensor'=4] {'frame'}, dimensions={1} | all-to-all | bytes 3538944 | tf_op jit(solution)/shard_map/all_to_all | solution.py:265
  1287.7 83.3 %reduce-scatter.35.cloned.1.call-done = f32[1,4,64,1152]{3,2,1,0:T(8,128)} async-done(((f32[1,4,256,1152]{3,2,1,0:T(8,128)}), f32[1,4,64,1152]{3,2,1,0:T(8,128)}) %reduce-scatter.35.cloned.1.call-update) | async-done | bytes 1179664 | tf_op jit(solution)/shard_map/reduce_scatter | solution.py:153
  1376.9 51.1 %all-gather.45.cloned.1.call-done = bf16[1,4,256,1152]{3,2,1,0:T(8,128)(2,1)} async-done(((bf16[1,4,64,1152]{3,2,1,0:T(8,128)(2,1)}), bf16[1,4,256,1152]{3,2,1,0:T(8,128)(2,1)}) %all-gather.45.cloned.1.call-update) | async-done | bytes 2359312 | tf_op jit(solution)/shard_map/all_gather | solution.py:149
  1442.3 84.2 %reduce-scatter.37.cloned.1.call-done = f32[1,4,64,1152]{3,2,1,0:T(8,128)} async-done(((f32[1,4,256,1152]{3,2,1,0:T(8,128)}), f32[1,4,64,1152]{3,2,1,0:T(8,128)}) %reduce-scatter.37.cloned.1.call-update) | async-done | bytes 1179664 | tf_op jit(solution)/shard_map/reduce_scatter | solution.py:153
  1532.8 50.7 %all-gather.47.cloned.1.call-done = bf16[1,4,256,1152]{3,2,1,0:T(8,128)(2,1)} async-done(((bf16[1,4,64,1152]{3,2,1,0:T(8,128)(2,1)}), bf16[1,4,256,1152]{3,2,1,0:T(8,128)(2,1)}) %all-gather.47.cloned.1.call-update) | async-done | bytes 2359312 | tf_op jit(solution)/shard_map/all_gather | solution.py:149
  1600.2 82.2 %reduce-scatter.39.cloned.1.call-done = f32[1,4,64,1152]{3,2,1,0:T(8,128)} async-done(((f32[1,4,256,1152]{3,2,1,0:T(8,128)}), f32[1,4,64,1152]{3,2,1,0:T(8,128)}) %reduce-scatter.39.cloned.1.call-update) | async-done | bytes 1179664 | tf_op jit(solution)/shard_map/reduce_scatter | solution.py:153
  1778.3 45.6 %reduce-scatter.59.cloned.1.call-done = bf16[1152,144]{0,1:T(8,128)(2,1)} async-done(((bf16[1152,1152]{0,1:T(8,128)(2,1)}), bf16[1152,144]{0,1:T(8,128)(2,1)}) %reduce-scatter.59.cloned.1.call-update) | async-done | bytes 331792 | tf_op jit(solution)/shard_map/reduce_scatter | solution.py:304
  1825.8 37.0 %reduce-scatter.55.cloned.1.call-done = bf16[288,144]{0,1:T(8,128)(2,1)} async-done(((bf16[288,1152]{0,1:T(8,128)(2,1)}), bf16[288,144]{0,1:T(8,128)(2,1)}) %reduce-scatter.55.cloned.1.call-update) | async-done | bytes 82960 | tf_op jit(solution)/shard_map/reduce_scatter | solution.py:298
  1864.4 46.1 %reduce-scatter.53.cloned.1.call-done = bf16[144,3,288]{2,0,1:T(8,128)(2,1)} async-done(((bf16[1152,3,288]{2,0,1:T(8,128)(2,1)}), bf16[144,3,288]{2,0,1:T(8,128)(2,1)}) %reduce-scatter.53.cloned.1.call-update) | async-done | bytes 248848 | tf_op jit(solution)/shard_map/reduce_scatter | solution.py:295
  1912.3 42.0 %all-gather.51.cloned.1.call-done = bf16[1152,6,288]{2,0,1:T(8,128)(2,1)} async-done(((bf16[144,6,288]{2,0,1:T(8,128)(2,1)}), bf16[1152,6,288]{2,0,1:T(8,128)(2,1)}) %all-gather.51.cloned.1.call-update) | async-done | bytes 3981328 | tf_op jit(solution)/shard_map/all_gather | solution.py:140
  1961.1 40.3 %reduce-scatter.49.cloned.1.call-done = bf16[1152,144]{0,1:T(8,128)(2,1)} async-done(((bf16[1152,1152]{0,1:T(8,128)(2,1)}), bf16[1152,144]{0,1:T(8,128)(2,1)}) %reduce-scatter.49.cloned.1.call-update) | async-done | bytes 331792 | tf_op jit(solution)/shard_map/reduce_scatter | solution.py:304
  2003.3 45.8 %reduce-scatter.47.cloned.1.call-done = bf16[144,1152]{1,0:T(8,128)(2,1)} async-done(((bf16[1152,1152]{1,0:T(8,128)(2,1)}), bf16[144,1152]{1,0:T(8,128)(2,1)}) %reduce-scatter.47.cloned.1.call-update) | async-done | bytes 331792 | tf_op jit(solution)/shard_map/reduce_scatter | solution.py:301
  2051.0 37.1 %reduce-scatter.45.cloned.1.call-done = bf16[288,144]{0,1:T(8,128)(2,1)} async-done(((bf16[288,1152]{0,1:T(8,128)(2,1)}), bf16[288,144]{0,1:T(8,128)(2,1)}) %reduce-scatter.45.cloned.1.call-update) | async-done | bytes 82960 | tf_op jit(solution)/shard_map/reduce_scatter | solution.py:298
  2089.7 45.9 %reduce-scatter.43.cloned.1.call-done = bf16[144,3,288]{2,0,1:T(8,128)(2,1)} async-done(((bf16[1152,3,288]{2,0,1:T(8,128)(2,1)}), bf16[144,3,288]{2,0,1:T(8,128)(2,1)}) %reduce-scatter.43.cloned.1.call-update) | async-done | bytes 248848 | tf_op jit(solution)/shard_map/reduce_scatter | solution.py:295
  2139.0 40.6 %all-gather.49.cloned.1.call-done = bf16[1152,6,288]{2,0,1:T(8,128)(2,1)} async-done(((bf16[144,6,288]{2,0,1:T(8,128)(2,1)}), bf16[1152,6,288]{2,0,1:T(8,128)(2,1)}) %all-gather.49.cloned.1.call-update) | async-done | bytes 3981328 | tf_op jit(solution)/shard_map/all_gather | solution.py:140
  2186.3 34.9 %psum.7 = f32[1,1152]{1,0:T(1,128)S(1)} all-reduce(f32[1,1152]{1,0:T(1,128)S(1)} %add.301), channel_id=1, replica_groups=mesh['clip'=2,'frame'=4,'tensor'=4] {'frame','tensor'}, use_global_device_ids=true, to_apply=%region_44.45 | all-reduce | flops 1152 | bytes 9216 | tf_op jit(solution)/shard_map/psum | solution.py:344
  2242.6 58.4 %reduce-scatter.51.cloned.1.call-done = bf16[144,6,288]{2,0,1:T(8,128)(2,1)} async-done(((bf16[1152,6,288]{2,0,1:T(8,128)(2,1)}), bf16[144,6,288]{2,0,1:T(8,128)(2,1)}) %reduce-scatter.51.cloned.1.call-update) | async-done | bytes 497680 | tf_op jit(solution)/shard_map/reduce_scatter | solution.py:292
  (478 shorter events, 598.2 us)
Async XLA Ops:
  7.2 174.9 %all-gather.23.cloned.1.call-start = ((), (), s32[]{:S(2)}) async-start(), calls=%async_computation.25 | async-start | bytes 2985984 | tf_op jit(solution)/shard_map/all_gather | solution.py:130
  83.9 138.8 %all-gather.21.cloned.1.call-start = ((), (), s32[]{:S(2)}) async-start(), calls=%async_computation.24 | async-start | bytes 2949120 | tf_op jit(solution)/shard_map/all_gather | solution.py:149
  171.1 148.5 %reduce-scatter.25.cloned.1.call-start = ((), (), s32[]{:S(2)}) async-start(), calls=%async_computation.26 | async-start | bytes 5898240 | tf_op jit(solution)/shard_map/reduce_scatter | solution.py:153
  235.3 117.4 %all-gather.27.cloned.1.call-start = ((), (), s32[]{:S(2)}) async-start(), calls=%async_computation.28 | async-start | bytes 2985984 | tf_op jit(solution)/shard_map/all_gather | solution.py:132
  237.2 168.0 %all-gather.25.cloned.1.call-start = ((), (), s32[]{:S(2)}) async-start(), calls=%async_computation.27 | async-start | bytes 2949120 | tf_op jit(solution)/shard_map/all_gather | solution.py:149
  323.5 208.9 %reduce-scatter.27.cloned.1.call-start = ((), (), s32[]{:S(2)}) async-start(), calls=%async_computation.30 | async-start | bytes 5898240 | tf_op jit(solution)/shard_map/reduce_scatter | solution.py:153
  446.2 119.4 %all-gather.33.cloned.1.call-start = ((), (), s32[]{:S(2)}) async-start(), calls=%async_computation.32 | async-start | bytes 2985984 | tf_op jit(solution)/shard_map/all_gather | solution.py:130
  452.2 166.0 %all-gather.31.cloned.1.call-start = ((), (), s32[]{:S(2)}) async-start(), calls=%async_computation.31 | async-start | bytes 2949120 | tf_op jit(solution)/shard_map/all_gather | solution.py:149
  704.4 116.8 %all-gather.37.cloned.1.call-start = ((), (), s32[]{:S(2)}) async-start(), calls=%async_computation.35 | async-start | bytes 2985984 | tf_op jit(solution)/shard_map/all_gather | solution.py:132
  706.4 167.3 %all-gather.35.cloned.1.call-start = ((), (), s32[]{:S(2)}) async-start(), calls=%async_computation.34 | async-start | bytes 2949120 | tf_op jit(solution)/shard_map/all_gather | solution.py:149
  793.5 164.2 %all-gather.41.cloned.1.call-start = ((), (), s32[]{:S(2)}) async-start(), calls=%async_computation.38 | async-start | bytes 2949120 | tf_op jit(solution)/shard_map/all_gather | solution.py:149
  795.6 260.7 %reduce-scatter.33.cloned.1.call-start = ((), (), s32[]{:S(2)}) async-start(), calls=%async_computation.39 | async-start | bytes 5898240 | tf_op jit(solution)/shard_map/reduce_scatter | solution.py:153
  972.0 172.2 %reduce-scatter.31.cloned.1.call-start = ((), (), s32[]{:S(2)}) async-start(), calls=%async_computation.37 | async-start | bytes 5898240 | tf_op jit(solution)/shard_map/reduce_scatter | solution.py:153
  981.7 220.3 %all-gather.43.cloned.1.call-start = ((), (), s32[]{:S(2)}) async-start(), calls=%async_computation.40 | async-start | bytes 2949120 | tf_op jit(solution)/shard_map/all_gather | solution.py:149
  1212.0 159.0 %reduce-scatter.35.cloned.1.call-start = ((), (), s32[]{:S(2)}) async-start(), calls=%async_computation.41 | async-start | bytes 5898240 | tf_op jit(solution)/shard_map/reduce_scatter | solution.py:153
  1287.6 140.3 %all-gather.45.cloned.1.call-start = ((), (), s32[]{:S(2)}) async-start(), calls=%async_computation.42 | async-start | bytes 2949120 | tf_op jit(solution)/shard_map/all_gather | solution.py:149
  1376.8 149.7 %reduce-scatter.37.cloned.1.call-start = ((), (), s32[]{:S(2)}) async-start(), calls=%async_computation.43 | async-start | bytes 5898240 | tf_op jit(solution)/shard_map/reduce_scatter | solution.py:153
  1442.2 141.2 %all-gather.47.cloned.1.call-start = ((), (), s32[]{:S(2)}) async-start(), calls=%async_computation.44 | async-start | bytes 2949120 | tf_op jit(solution)/shard_map/all_gather | solution.py:149
  1532.3 150.1 %reduce-scatter.39.cloned.1.call-start = ((), (), s32[]{:S(2)}) async-start(), calls=%async_computation.45 | async-start | bytes 5898240 | tf_op jit(solution)/shard_map/reduce_scatter | solution.py:153
  1598.1 148.1 %reduce-scatter.63.cloned.1.call-start = ((), (), s32[]{:S(2)}) async-start(), calls=%async_computation.59 | async-start | bytes 737280
  1600.1 147.1 %reduce-scatter.61.cloned.1.call-start = ((), (), s32[]{:S(2)}) async-start(), calls=%async_computation.58 | async-start | bytes 737280
  1693.4 130.6 %reduce-scatter.59.cloned.1.call-start = ((), (), s32[]{:S(2)}) async-start(), calls=%async_computation.57 | async-start | bytes 2985984 | tf_op jit(solution)/shard_map/reduce_scatter | solution.py:304
  1701.6 161.1 %reduce-scatter.55.cloned.1.call-start = ((), (), s32[]{:S(2)}) async-start(), calls=%async_computation.55 | async-start | bytes 995328 | tf_op jit(solution)/shard_map/reduce_scatter | solution.py:298
  1706.8 203.7 %reduce-scatter.53.cloned.1.call-start = ((), (), s32[]{:S(2)}) async-start(), calls=%async_computation.54 | async-start | bytes 2985984 | tf_op jit(solution)/shard_map/reduce_scatter | solution.py:295
  1714.0 240.3 %all-gather.51.cloned.1.call-start = ((), (), s32[]{:S(2)}) async-start(), calls=%async_computation.47 | async-start | bytes 5971968 | tf_op jit(solution)/shard_map/all_gather | solution.py:140
  1716.3 285.1 %reduce-scatter.49.cloned.1.call-start = ((), (), s32[]{:S(2)}) async-start(), calls=%async_computation.52 | async-start | bytes 2985984 | tf_op jit(solution)/shard_map/reduce_scatter | solution.py:304
  1724.4 324.7 %reduce-scatter.47.cloned.1.call-start = ((), (), s32[]{:S(2)}) async-start(), calls=%async_computation.51 | async-start | bytes 2985984 | tf_op jit(solution)/shard_map/reduce_scatter | solution.py:301
  1731.8 356.3 %reduce-scatter.45.cloned.1.call-start = ((), (), s32[]{:S(2)}) async-start(), calls=%async_computation.50 | async-start | bytes 995328 | tf_op jit(solution)/shard_map/reduce_scatter | solution.py:298
  1736.9 398.7 %reduce-scatter.43.cloned.1.call-start = ((), (), s32[]{:S(2)}) async-start(), calls=%async_computation.49 | async-start | bytes 2985984 | tf_op jit(solution)/shard_map/reduce_scatter | solution.py:295
  1743.8 435.7 %all-gather.49.cloned.1.call-start = ((), (), s32[]{:S(2)}) async-start(), calls=%async_computation.46 | async-start | bytes 5971968 | tf_op jit(solution)/shard_map/all_gather | solution.py:140
  1746.1 494.3 %reduce-scatter.41.cloned.1.call-start = ((), (), s32[]{:S(2)}) async-start(), calls=%async_computation.48 | async-start | bytes 5971968 | tf_op jit(solution)/shard_map/reduce_scatter | solution.py:292
  1755.1 545.9 %reduce-scatter.51.cloned.1.call-start = ((), (), s32[]{:S(2)}) async-start(), calls=%async_computation.53 | async-start | bytes 5971968 | tf_op jit(solution)/shard_map/reduce_scatter | solution.py:292
  (113 other events, 4460.6 us)
Sparse Core Ops, SparseCore 0:
  84.0 41.4 all-gather.22
  171.2 51.4 all-gather.20
  235.4 84.0 reduce-scatter.24
  321.9 30.7 all-gather.26
  354.7 50.4 all-gather.24
  446.3 85.9 reduce-scatter.26
  534.8 30.7 all-gather.32
  567.7 50.4 all-gather.30
  704.6 83.3 reduce-scatter.28
  790.4 30.7 all-gather.36
  823.2 50.4 all-gather.34
  907.3 50.4 all-gather.40
  972.2 84.0 reduce-scatter.32
  1058.4 85.7 reduce-scatter.30
  1151.0 50.9 all-gather.42
  1287.8 83.1 reduce-scatter.34
  1376.9 50.9 all-gather.44
  1442.4 84.0 reduce-scatter.36
  1532.4 50.9 all-gather.46
  1598.3 84.0 reduce-scatter.38
  1734.3 42.1 reduce-scatter.56
  1780.2 43.7 reduce-scatter.58
  1827.6 35.1 reduce-scatter.54
  1866.7 43.7 reduce-scatter.52
  1912.9 41.3 all-gather.50
  1957.7 43.7 reduce-scatter.48
  2005.4 43.7 reduce-scatter.46
  2052.9 35.1 reduce-scatter.44
  2091.8 43.7 reduce-scatter.42
  2138.1 41.3 all-gather.48
  2183.0 57.3 reduce-scatter.40
  2243.8 57.2 reduce-scatter.50
  (4 shorter events, 100.7 us)
